TPU v7x, 32 devices: a whole 2x2x4 slice. The times are simulated.
32 devices in a mesh: layer: 2 (over y), latent: 8 (over z, x), tok: 2 (over core).
Axes of the slice: x: 2, y: 2, z: 4, core: 2. Of those that a mesh axis runs over, the one named last changes fastest.
Arguments:
- resid: bfloat16 [2, 384, 2304], P('layer', 'tok', 'latent'), may hold values from -6 to 6
- w_enc: bfloat16 [2, 2304, 2048], P('layer', None, 'latent'), may hold values from -0.09375 to 0.09375
- b_enc: float32 [2048], P('latent'), may hold values from -3 to 3
- w_dec: bfloat16 [2, 2048, 2304], P('layer', 'latent'), may hold values from -0.125 to 0.125
- b_dec: bfloat16 [2, 2304], P('layer', 'latent'), may hold values from -3 to 3
Outputs:
- grad_w_enc: bfloat16 [2, 2304, 2048], P('layer', 'tok', 'latent')
- grad_w_dec: bfloat16 [2, 2048, 2304], P('layer', 'latent')
All inputs are finite; a program needn't handle non-finite values.
Results may differ from a plain program's by a relative error of at most 0.023.
Values may be sent and summed in bfloat16 or wider, within the bound.
A program may use at most 64 MiB of HBM per device.

v0:
```python
import jax
import jax.numpy as jnp
from jax import lax
from jax.sharding import PartitionSpec as P

BETA = 4.0


def shards(resid, w_enc, b_enc, w_dec, b_dec):
    decoder = w_dec[0]
    x_full, bias_full = (
        lax.all_gather(resid, "latent", axis=2, tiled=True),
        lax.all_gather(b_dec.reshape(1, 1, -1), "latent", axis=2, tiled=True),
    )
    x_full = x_full[0]
    bias_full = bias_full.reshape(-1).astype(jnp.float32)
    tok_rows = x_full.shape[0]
    tokens = tok_rows * lax.axis_size("tok")
    partial_value = jnp.dot(x_full, w_enc[0], preferred_element_type=jnp.float32)
    pre = lax.psum(partial_value.astype(jnp.bfloat16), "layer").astype(jnp.float32) + b_enc
    act = (jax.nn.softplus(BETA * pre) / BETA).astype(jnp.bfloat16)
    slope = jax.nn.sigmoid(BETA * pre)
    recon = lax.psum(
        jnp.dot(act, decoder, preferred_element_type=jnp.float32).astype(jnp.bfloat16), "latent"
    ).astype(jnp.float32)
    grad_all = (2.0 / tokens * (recon + bias_full - x_full.astype(jnp.float32))).astype(
        jnp.bfloat16
    )
    dec_sum = lax.dot_general(
        act, grad_all, (((0,), (0,)), ((), ())), preferred_element_type=jnp.float32
    )
    rows_grad = lax.dot_general(
        grad_all, decoder, (((1,), (1,)), ((), ())), preferred_element_type=jnp.float32
    )
    act_grad = rows_grad
    dec_sum, act_grad = (dec_sum, act_grad)
    grad_act = lax.psum(act_grad.astype(jnp.bfloat16), "layer").astype(jnp.float32)
    grad_pre = (grad_act * slope).astype(jnp.bfloat16)
    grad_w_dec = lax.psum(dec_sum.astype(jnp.bfloat16), "tok")
    grad_w_enc = lax.psum_scatter(
        lax.dot_general(
            x_full, grad_pre, (((0,), (0,)), ((), ())), preferred_element_type=jnp.float32
        ).astype(jnp.bfloat16),
        "tok",
        scatter_dimension=0,
        tiled=True,
    )
    return (grad_w_enc[None], grad_w_dec[None])


def solution(mesh):
    placed = (
        P("layer", "tok", "latent"),
        P("layer", None, "latent"),
        P("latent"),
        P("layer", "latent", None),
        P("layer", "latent"),
    )
    return jax.shard_map(
        shards,
        mesh=mesh,
        in_specs=placed,
        out_specs=(P("layer", "tok", "latent"), P("layer", "latent", None)),
        check_vma=False,
    )
```

profile of v0, /device:TPU:0, one launch (start us, length us, event | category | flops | bytes accessed | tf_op | source)
XLA Modules:
  0.0 235.1 jit_solution(12181217095717214668)
XLA Ops:
  7.2 0.0 copy-start
  7.2 0.0 all-reduce.6.cloned.1.call-start
  7.2 1.9 copy.8
  9.1 51.7 %all_gather.6 = bf16[1,192,2304]{1,0,2:T(2,128)(2,1)S(1)} all-gather(bf16[1,192,288]{1,0,2:T(2,128)(2,1)} %copy.8), channel_id=1, replica_groups=mesh['layer'=2,'latent'=8,'tok'=2] {'latent'}, dimensions={2}, use_global_device_ids=true | all-gather | bytes 995328 | tf_op jit(solution)/shard_map/all_gather | solution.py:12
  60.8 4.9 %copy.9 = bf16[1,192,2304]{2,1,0:T(8,128)(2,1)} copy(bf16[1,192,2304]{1,0,2:T(2,128)(2,1)S(1)} %all_gather.6) | data formatting | bytes 1769472 | tf_op jit(solution)/shard_map/all_gather | solution.py:12
  65.7 2.6 %fusion.7 = bf16[192,256]{1,0:T(8,128)(2,1)} fusion(bf16[1,2304,256]{2,1,0:T(8,128)(2,1)} %param.6, bf16[1,192,2304]{2,1,0:T(8,128)(2,1)} %copy.9), kind=kOutput, calls=%fused_computation.11 | convolution fusion | flops 226541568 | bytes 2162688 | tf_op jit(solution)/shard_map/dot_general | solution.py:19
  68.3 0.0 all-reduce.6.cloned.1.call-update
  68.3 0.0 all-reduce.8.cloned.1.call-start
  68.4 20.0 %all-reduce.6.cloned.1.call-done = bf16[192,256]{1,0:T(8,128)(2,1)} async-done(((bf16[192,256]{1,0:T(8,128)(2,1)}), bf16[192,256]{1,0:T(8,128)(2,1)}) %all-reduce.6.cloned.1.call-update) | async-done | bytes 98320 | tf_op jit(solution)/shard_map/psum | solution.py:20
  88.3 0.0 copy-done
  88.3 2.3 convolution_convert_fusion.2
  90.7 0.0 all-reduce.8.cloned.1.call-update
  90.7 0.0 all-reduce.10.cloned.1.call-start
  90.7 0.6 dynamic-slice
  92.0 0.3 dynamic-update-slice
  92.3 22.1 %all-reduce = bf16[2304]{0:T(1024)(128)(2,1)S(1)} all-reduce(bf16[2304]{0:T(1024)(128)(2,1)S(1)} %dynamic-update-slice), channel_id=2, replica_groups=mesh['layer'=2,'latent'=8,'tok'=2] {'latent'}, use_global_device_ids=true, to_apply=%add | all-reduce | flops 2304 | bytes 9216
  114.4 53.9 %all-reduce.8.cloned.1.call-done = bf16[192,2304]{1,0:T(8,128)(2,1)} async-done(((bf16[192,2304]{1,0:T(8,128)(2,1)}), bf16[192,2304]{1,0:T(8,128)(2,1)}) %all-reduce.8.cloned.1.call-update) | async-done | bytes 884752 | tf_op jit(solution)/shard_map/psum | solution.py:23
  168.3 2.4 %fusion.10 = bf16[192,256]{1,0:T(8,128)(2,1)} fusion(bf16[1,256,2304]{2,1,0:T(8,128)(2,1)S(1)} %copy-done, bf16[192,2304]{1,0:T(8,128)(2,1)} %all-reduce.8.cloned.1.call-done, bf16[1,192,2304]{2,1,0:T(8,128)(2,1)S(1)} %copy-done.1, f32[2304]{0:T(1024)S(1)} %convert_element_type.66), kind=kOutput, calls=%fused_computation.12 | convolution fusion | flops 229195776 | bytes 3056640 | tf_op jit(solution)/shard_map/dot_general | solution.py:32
  170.7 0.0 all-reduce.10.cloned.1.call-update
  170.7 0.0 reduce-scatter.4.cloned.1.call-start
  170.8 20.7 %all-reduce.10.cloned.1.call-done = bf16[192,256]{1,0:T(8,128)(2,1)} async-done(((bf16[192,256]{1,0:T(8,128)(2,1)}), bf16[192,256]{1,0:T(8,128)(2,1)}) %all-reduce.10.cloned.1.call-update) | async-done | bytes 98320 | tf_op jit(solution)/shard_map/psum | solution.py:37
  191.4 1.4 fusion
  192.9 1.4 copy.11
  194.3 0.0 reduce-scatter.4.cloned.1.call-update
  194.3 0.0 all-reduce.12.cloned.1.call-start
  194.4 2.9 %fusion.1 = bf16[1,256,2304]{2,1,0:T(8,128)(2,1)} fusion(bf16[192,2304]{1,0:T(8,128)(2,1)} %all-reduce.8.cloned.1.call-done, bf16[1,192,2304]{2,1,0:T(8,128)(2,1)S(1)} %copy-done.1, f32[2304]{0:T(1024)S(1)} %convert_element_type.66, bf16[192,256]{1,0:T(8,128)(2,1)S(1)} %copy-done.2, f32[256]{0:T(256)S(1)} %copy-done.4), kind=kOutput, calls=%fused_computation.4 | convolution fusion | flops 230277120 | bytes 3057664 | tf_op jit(solution)/shard_map/dot_general | solution.py:29
  197.3 0.0 all-reduce.12.cloned.1.call-update
  197.3 5.7 %reduce-scatter.4.cloned.1.call-done = bf16[1152,256]{1,0:T(8,128)(2,1)} async-done(((bf16[2304,256]{1,0:T(8,128)(2,1)}), bf16[1152,256]{1,0:T(8,128)(2,1)}) %reduce-scatter.4.cloned.1.call-update) | async-done | bytes 589840
  203.0 1.4 copy.12
  204.4 1.1 copy.10
  205.4 20.7 %all-reduce.12.cloned.1.call-done = bf16[1,256,2304]{2,1,0:T(8,128)(2,1)} async-done(((bf16[1,256,2304]{2,1,0:T(8,128)(2,1)}), bf16[1,256,2304]{2,1,0:T(8,128)(2,1)}) %all-reduce.12.cloned.1.call-update) | async-done | bytes 1179664 | tf_op jit(solution)/shard_map/psum | solution.py:39
  226.2 2.4 %copy.18 = bf16[1,256,2304]{2,1,0:T(8,128)(2,1)} copy(bf16[1,256,2304]{2,1,0:T(8,128)(2,1)} %all-reduce.12.cloned.1.call-done) | data formatting | bytes 2359296
  (13 shorter events, 0.0 us)
Async XLA Ops:
  7.2 81.2 %copy-start = (bf16[1,256,2304]{2,1,0:T(8,128)(2,1)S(1)}, bf16[1,256,2304]{2,1,0:T(8,128)(2,1)}, u32[]{:S(2)}) copy-start(bf16[1,256,2304]{2,1,0:T(8,128)(2,1)} %param.8) | copy-start | bytes 3538948
  7.2 81.2 %all-reduce.6.cloned.1.call-start = ((), (), s32[]{:S(2)}) async-start(), calls=%async_computation.1 | async-start | bytes 196608 | tf_op jit(solution)/shard_map/psum | solution.py:20
  65.7 22.7 %copy-start.4 = (f32[256]{0:T(256)S(1)}, f32[256]{0:T(256)}, u32[]{:S(2)}) copy-start(f32[256]{0:T(256)} %param.7) | copy-start | bytes 3076
  68.3 22.5 %copy-start.5 = (u32[32]{0:T(128)S(1)}, u32[32]{0:T(128)}, u32[]{:S(2)}) copy-start(u32[32]{0:T(128)} %constant.17) | copy-start | bytes 388
  68.3 23.7 %copy-start.3 = (bf16[1,288]{1,0:T(2,128)(2,1)S(1)}, bf16[1,288]{1,0:T(2,128)(2,1)}, u32[]{:S(2)}) copy-start(bf16[1,288]{1,0:T(2,128)(2,1)} %param.9) | copy-start | bytes 1732
  68.3 100.0 %copy-start.1 = (bf16[1,192,2304]{2,1,0:T(8,128)(2,1)S(1)}, bf16[1,192,2304]{2,1,0:T(8,128)(2,1)}, u32[]{:S(2)}) copy-start(bf16[1,192,2304]{2,1,0:T(8,128)(2,1)} %copy.9) | copy-start | bytes 2654212
  68.3 100.0 %all-reduce.8.cloned.1.call-start = ((), (), s32[]{:S(2)}) async-start(), calls=%async_computation.2 | async-start | bytes 1769472 | tf_op jit(solution)/shard_map/psum | solution.py:23
  90.7 100.7 %all-reduce.10.cloned.1.call-start = ((), (), s32[]{:S(2)}) async-start(), calls=%async_computation.3 | async-start | bytes 196608 | tf_op jit(solution)/shard_map/psum | solution.py:37
  114.4 77.0 %copy-start.2 = (bf16[192,256]{1,0:T(8,128)(2,1)S(1)}, bf16[192,256]{1,0:T(8,128)(2,1)}, u32[]{:S(2)}) copy-start(bf16[192,256]{1,0:T(8,128)(2,1)} %all-reduce.6.cloned.1.call-done) | copy-start | bytes 294916
  170.7 32.3 %reduce-scatter.4.cloned.1.call-start = ((), (), s32[]{:S(2)}) async-start(), calls=%async_computation.5 | async-start | bytes 1769472
  194.3 31.8 %all-reduce.12.cloned.1.call-start = ((), (), s32[]{:S(2)}) async-start(), calls=%async_computation.4 | async-start | bytes 2359296 | tf_op jit(solution)/shard_map/psum | solution.py:39
Sparse Core Ops, SparseCore 0:
  68.4 19.8 all-reduce.5
  91.8 76.4 all-reduce.7
  171.1 20.2 all-reduce.9
  194.4 8.5 reduce-scatter.3
  205.2 20.9 all-reduce.11
where the time goes:
time: 235 us
  waiting for transfers between devices  121 us (51%)
  blocking collectives  73.7 us (31%)
  between operations  14.5 us (6%)
  local copies, waits for them, and re-layouts  13.9 us (6%)
  matrix products  11.6 us (5%)
    psum x1, waiting for transfers between devices, shards(): lax.psum(jnp.dot(act, decoder, preferred_element_type=jnp.float32).astype...  53.9 us
    all_gather x1, blocking collectives, shards(): lax.all_gather(resid, 'latent', axis=2, tiled=True)  51.7 us
    unnamed x1, blocking collectives  22.1 us
    psum x1, waiting for transfers between devices, shards(): grad_w_dec = lax.psum(dec_sum.astype(jnp.bfloat16), 'tok')  20.7 us
    psum x1, waiting for transfers between devices, shards(): lax.psum(act_grad.astype(jnp.bfloat16), 'layer').astype(jnp.float32)  20.7 us
    psum x1, waiting for transfers between devices, shards(): lax.psum(partial_value.astype(jnp.bfloat16), 'layer').astype(jnp.float32)  20 us
    unnamed x20, local copies, waits for them, and re-layouts  8.98 us
    unnamed x6, waiting for transfers between devices  5.8 us
  transfers between devices with their start and end apart: 5, of which 5 were waited for; matrix products, arithmetic and copies ran while one was open for 3% of the time, Pallas kernels for 0%

commit v1 on v0

--- a/solution.py
+++ b/solution.py
@@ -8,8 +8,9 @@
 
 def shards(resid, w_enc, b_enc, w_dec, b_dec):
     decoder = w_dec[0]
+    hold_the_sums_all = lambda page: jnp.concatenate(lax.all_gather(page, "latent"), 2)
     x_full, bias_full = (
-        lax.all_gather(resid, "latent", axis=2, tiled=True),
+        hold_the_sums_all(resid),
         lax.all_gather(b_dec.reshape(1, 1, -1), "latent", axis=2, tiled=True),
     )
     x_full = x_full[0]

time: 235 us -> 216 us (0.919)
  blocking collectives: 73.7 us -> 57.8 us
  local copies, waits for them, and re-layouts: 13.9 us -> 9.75 us
    all_gather x1, blocking collectives: 51.7 us -> 35.7 us  [shards(): lax.all_gather(page, 'latent')]
    all_gather x1 -> x0, local copies, waits for them, and re-layouts: 4.88 us -> none  [shards(): lax.all_gather(resid, 'latent', axis=2, tiled=True)]
    unnamed x20 -> x19, local copies, waits for them, and re-layouts: 8.98 us -> 8.17 us
  transfers between devices with their start and end apart: 5 -> 5, of which waited for: 5 -> 5; matrix products, arithmetic and copies ran while one was open for 3% -> 2% of each run, Pallas kernels for 0% -> 0%
where the time goes in v1:
time: 216 us
  waiting for transfers between devices  123 us (57%)
  blocking collectives  57.8 us (27%)
  between operations  14.5 us (7%)
  matrix products  10.2 us (5%)
  local copies, waits for them, and re-layouts  9.75 us (5%)
    psum x1, waiting for transfers between devices, shards(): lax.psum(jnp.dot(act, decoder, preferred_element_type=jnp.float32).astype...  54.2 us
    all_gather x1, blocking collectives, shards(): lax.all_gather(page, 'latent')  35.7 us
    unnamed x1, blocking collectives  22.1 us
    psum x1, waiting for transfers between devices, shards(): lax.psum(partial_value.astype(jnp.bfloat16), 'layer').astype(jnp.float32)  21.7 us
    psum x1, waiting for transfers between devices, shards(): grad_w_dec = lax.psum(dec_sum.astype(jnp.bfloat16), 'tok')  20.7 us
    psum x1, waiting for transfers between devices, shards(): lax.psum(act_grad.astype(jnp.bfloat16), 'layer').astype(jnp.float32)  20.7 us
    unnamed x19, local copies, waits for them, and re-layouts  8.17 us
    unnamed x6, waiting for transfers between devices  5.83 us
  transfers between devices with their start and end apart: 5, of which 5 were waited for; matrix products, arithmetic and copies ran while one was open for 2% of the time, Pallas kernels for 0%

profile of v1, /device:TPU:0, one launch (start us, length us, event | category | flops | bytes accessed | tf_op | source)
XLA Modules:
  0.0 215.6 jit_solution(6829175169416253188)
XLA Ops:
  7.2 0.0 copy-start
  7.2 0.0 all-reduce.6.cloned.1.call-start
  7.2 35.7 %all-gather = bf16[8,192,288]{2,1,0:T(8,128)(2,1)S(1)} all-gather(bf16[1,192,288]{2,1,0:T(8,128)(2,1)} %param.5), channel_id=2, replica_groups=mesh['layer'=2,'latent'=8,'tok'=2] {'latent'}, dimensions={0}, use_global_device_ids=true | all-gather | bytes 995328 | tf_op jit(solution)/shard_map/all_gather | solution.py:11
  42.9 0.7 copy.9
  43.6 0.9 squeeze_reshape.3
  44.5 2.3 %fusion.7 = bf16[192,256]{1,0:T(8,128)(2,1)} fusion(bf16[192,2304]{1,0:T(8,128)(2,1)S(1)} %squeeze_reshape.3, bf16[1,2304,256]{2,1,0:T(8,128)(2,1)} %param.6), kind=kOutput, calls=%fused_computation.11 | convolution fusion | flops 226541568 | bytes 2162688 | tf_op jit(solution)/shard_map/dot_general | solution.py:20
  46.9 0.0 all-reduce.6.cloned.1.call-update
  46.9 0.0 all-reduce.8.cloned.1.call-start
  47.0 21.7 %all-reduce.6.cloned.1.call-done = bf16[192,256]{1,0:T(8,128)(2,1)} async-done(((bf16[192,256]{1,0:T(8,128)(2,1)}), bf16[192,256]{1,0:T(8,128)(2,1)}) %all-reduce.6.cloned.1.call-update) | async-done | bytes 98320 | tf_op jit(solution)/shard_map/psum | solution.py:21
  68.6 2.3 %convolution_convert_fusion.2 = bf16[192,2304]{1,0:T(8,128)(2,1)} fusion(bf16[1,256,2304]{2,1,0:T(8,128)(2,1)S(1)} %copy-done, bf16[192,256]{1,0:T(8,128)(2,1)} %all-reduce.6.cloned.1.call-done, f32[256]{0:T(256)S(1)} %copy-done.3), kind=kOutput, calls=%fused_computation.2 | convolution fusion | flops 227475456 | bytes 2163712 | tf_op jit(solution)/shard_map/dot_general | solution.py:25
  70.9 0.0 all-reduce.8.cloned.1.call-update
  71.0 0.0 all-reduce.10.cloned.1.call-start
  71.0 0.6 dynamic-slice
  72.3 0.3 dynamic-update-slice
  72.6 22.1 %all-reduce = bf16[2304]{0:T(1024)(128)(2,1)S(1)} all-reduce(bf16[2304]{0:T(1024)(128)(2,1)S(1)} %dynamic-update-slice), channel_id=3, replica_groups=mesh['layer'=2,'latent'=8,'tok'=2] {'latent'}, use_global_device_ids=true, to_apply=%add | all-reduce | flops 2304 | bytes 9216
  94.7 54.2 %all-reduce.8.cloned.1.call-done = bf16[192,2304]{1,0:T(8,128)(2,1)} async-done(((bf16[192,2304]{1,0:T(8,128)(2,1)}), bf16[192,2304]{1,0:T(8,128)(2,1)}) %all-reduce.8.cloned.1.call-update) | async-done | bytes 884752 | tf_op jit(solution)/shard_map/psum | solution.py:24
  148.9 2.4 %fusion.10 = bf16[192,256]{1,0:T(8,128)(2,1)} fusion(bf16[1,256,2304]{2,1,0:T(8,128)(2,1)S(1)} %copy-done, bf16[192,2304]{1,0:T(8,128)(2,1)S(1)} %squeeze_reshape.3, bf16[192,2304]{1,0:T(8,128)(2,1)} %all-reduce.8.cloned.1.call-done, f32[2304]{0:T(1024)S(1)} %convert_element_type.66), kind=kOutput, calls=%fused_computation.12 | convolution fusion | flops 229195776 | bytes 3056640 | tf_op jit(solution)/shard_map/dot_general | solution.py:33
  151.3 0.0 all-reduce.10.cloned.1.call-update
  151.3 0.0 reduce-scatter.4.cloned.1.call-start
  151.4 20.7 %all-reduce.10.cloned.1.call-done = bf16[192,256]{1,0:T(8,128)(2,1)} async-done(((bf16[192,256]{1,0:T(8,128)(2,1)}), bf16[192,256]{1,0:T(8,128)(2,1)}) %all-reduce.10.cloned.1.call-update) | async-done | bytes 98320 | tf_op jit(solution)/shard_map/psum | solution.py:38
  172.0 1.4 fusion
  173.5 1.4 copy.11
  174.9 0.0 reduce-scatter.4.cloned.1.call-update
  174.9 0.0 all-reduce.12.cloned.1.call-start
  175.0 1.1 copy-done.4
  176.1 1.8 fusion.1
  177.8 0.0 all-reduce.12.cloned.1.call-update
  177.8 5.7 %reduce-scatter.4.cloned.1.call-done = bf16[1152,256]{1,0:T(8,128)(2,1)} async-done(((bf16[2304,256]{1,0:T(8,128)(2,1)}), bf16[1152,256]{1,0:T(8,128)(2,1)}) %reduce-scatter.4.cloned.1.call-update) | async-done | bytes 589840
  183.6 1.4 copy.12
  184.9 1.1 copy.10
  186.0 20.7 %all-reduce.12.cloned.1.call-done = bf16[1,256,2304]{2,1,0:T(8,128)(2,1)} async-done(((bf16[1,256,2304]{2,1,0:T(8,128)(2,1)}), bf16[1,256,2304]{2,1,0:T(8,128)(2,1)}) %all-reduce.12.cloned.1.call-update) | async-done | bytes 1179664 | tf_op jit(solution)/shard_map/psum | solution.py:40
  206.8 2.4 %copy.18 = bf16[1,256,2304]{2,1,0:T(8,128)(2,1)} copy(bf16[1,256,2304]{2,1,0:T(8,128)(2,1)} %all-reduce.12.cloned.1.call-done) | data formatting | bytes 2359296
  (13 shorter events, 0.1 us)
Async XLA Ops:
  7.2 61.5 %copy-start = (bf16[1,256,2304]{2,1,0:T(8,128)(2,1)S(1)}, bf16[1,256,2304]{2,1,0:T(8,128)(2,1)}, u32[]{:S(2)}) copy-start(bf16[1,256,2304]{2,1,0:T(8,128)(2,1)} %param.8) | copy-start | bytes 3538948
  7.2 61.5 %all-reduce.6.cloned.1.call-start = ((), (), s32[]{:S(2)}) async-start(), calls=%async_computation.1 | async-start | bytes 196608 | tf_op jit(solution)/shard_map/psum | solution.py:21
  44.5 24.1 %copy-start.3 = (f32[256]{0:T(256)S(1)}, f32[256]{0:T(256)}, u32[]{:S(2)}) copy-start(f32[256]{0:T(256)} %param.7) | copy-start | bytes 3076
  46.9 24.1 %copy-start.5 = (u32[32]{0:T(128)S(1)}, u32[32]{0:T(128)}, u32[]{:S(2)}) copy-start(u32[32]{0:T(128)} %constant.17) | copy-start | bytes 388
  46.9 25.4 %copy-start.2 = (bf16[1,288]{1,0:T(2,128)(2,1)S(1)}, bf16[1,288]{1,0:T(2,128)(2,1)}, u32[]{:S(2)}) copy-start(bf16[1,288]{1,0:T(2,128)(2,1)} %param.9) | copy-start | bytes 1732
  46.9 102.0 %all-reduce.8.cloned.1.call-start = ((), (), s32[]{:S(2)}) async-start(), calls=%async_computation.2 | async-start | bytes 1769472 | tf_op jit(solution)/shard_map/psum | solution.py:24
  71.0 101.1 %all-reduce.10.cloned.1.call-start = ((), (), s32[]{:S(2)}) async-start(), calls=%async_computation.3 | async-start | bytes 196608 | tf_op jit(solution)/shard_map/psum | solution.py:38
  94.7 77.3 %copy-start.1 = (bf16[192,256]{1,0:T(8,128)(2,1)S(1)}, bf16[192,256]{1,0:T(8,128)(2,1)}, u32[]{:S(2)}) copy-start(bf16[192,256]{1,0:T(8,128)(2,1)} %all-reduce.6.cloned.1.call-done) | copy-start | bytes 294916
  151.3 32.3 %reduce-scatter.4.cloned.1.call-start = ((), (), s32[]{:S(2)}) async-start(), calls=%async_computation.5 | async-start | bytes 1769472
  174.9 1.2 copy-start.4
  174.9 31.8 %all-reduce.12.cloned.1.call-start = ((), (), s32[]{:S(2)}) async-start(), calls=%async_computation.4 | async-start | bytes 2359296 | tf_op jit(solution)/shard_map/psum | solution.py:40
Sparse Core Ops, SparseCore 0:
  47.0 21.5 all-reduce.5
  72.7 76.2 all-reduce.7
  151.7 20.2 all-reduce.9
  175.0 8.5 reduce-scatter.3
  185.8 20.9 all-reduce.11
